TPU v7x, 256 devices: a whole 4x4x8 slice. The times are simulated.
256 devices in a mesh: rows: 16 (over z, core), cols: 16 (over y, x).
Axes of the slice: x: 4, y: 4, z: 8, core: 2. Of those that a mesh axis runs over, the one named last changes fastest.
Arguments:
- window_slab: float32 [24576, 4096], P('rows', 'cols'), may hold values from -6 to 6
- first_inverse: float32 [2, 512, 512], replicated, may hold values from -2 to 2, as said below
- first_factor: float32 [2, 512, 24576], P(None, 'cols', 'rows'), may hold values from -0.25 to 0.25
- second_inverse: float32 [2, 512, 512], replicated, may hold values from -2 to 2, as said below
- second_factor: float32 [2, 512, 4096], P(None, 'cols', 'rows'), may hold values from -0.25 to 0.25
Outputs:
- reduced: float32 [24576, 4096], P('cols', 'rows')
Inputs may be any that keep to these rules, and one draw needn't show every extreme that they name: first_inverse[k] is lower triangular with diagonal entries from 0.5 to 2. second_inverse[k] is lower triangular with diagonal entries from 0.5 to 2.
All inputs are finite; a program needn't handle non-finite values.
Results may differ from a plain program's by a relative error of at most 0.0001.
Values sent between devices are 32-bit elements; how exact they have to be, the bound alone decides.
A program may use at most 64 MiB of HBM per device.

v0:
```python
import jax
import jax.numpy as jnp
from jax import lax
from jax.sharding import PartitionSpec as P

BLOCK = 128
HIGHEST = lax.Precision.HIGHEST
CONTRACT_ROWS = (((0,), (0,)), ((), ()))
CONTRACT_COLS = (((1,), (1,)), ((), ()))


def right_solve(current, first_column, inverses, total_of, update_of):
    height, breadth = current.shape
    panel_count = inverses.shape[0]
    panel_width = inverses.shape[1]
    portion = min(breadth, panel_width)
    columns = first_column + lax.broadcasted_iota(jnp.int32, (1, breadth), 1)
    for panel_index in range(panel_count):
        panel_start = panel_index * panel_width
        panel_end = panel_start + panel_width
        inner_offset = jnp.clip(first_column - panel_start, 0, panel_width - portion)
        member = jnp.logical_and(first_column < panel_end, first_column + breadth > panel_start)
        own_columns = current
        inverse_cols = lax.dynamic_slice_in_dim(inverses[panel_index], inner_offset, portion, 1)
        partial_value = lax.dot_general(
            own_columns,
            inverse_cols,
            CONTRACT_COLS,
            precision=HIGHEST,
            preferred_element_type=jnp.float32,
        )
        solved = total_of(jnp.where(member, partial_value, 0.0))
        update = update_of(panel_index, solved)
        current = jnp.where(columns >= panel_end, current - update, current)
        mine_cols = lax.dynamic_slice_in_dim(solved, inner_offset, portion, 1)
        present = current
        current = jnp.where(member, mine_cols, present)
    return current


def on_device(window_slab, first_inverse, first_factor, second_inverse, second_factor):
    row_count = lax.axis_size("rows")
    row_index = lax.axis_index("rows")
    row_share, breadth = window_slab.shape
    panel_count = first_inverse.shape[0]
    panel_width = first_inverse.shape[1]
    blocks_per_panel = panel_width // BLOCK
    local_rows = lax.broadcasted_iota(jnp.int32, (row_share, 1), 0)
    logical_rows = (local_rows // BLOCK * row_count + row_index) * BLOCK + local_rows % BLOCK
    current = window_slab
    for panel_index in range(panel_count):
        panel_start = panel_index * panel_width
        panel_end = panel_start + panel_width
        local_block = panel_start // (row_count * BLOCK)
        first_group = panel_start // BLOCK % row_count
        member = jnp.logical_and(
            row_index >= first_group, row_index < first_group + blocks_per_panel
        )
        offset = jnp.clip(row_index - first_group, 0, blocks_per_panel - 1) * BLOCK
        own_rows = current[local_block * BLOCK : (local_block + 1) * BLOCK]
        inverse_cols = lax.dynamic_slice_in_dim(first_inverse[panel_index], offset, BLOCK, 1)
        partial_value = jnp.dot(
            inverse_cols, own_rows, precision=HIGHEST, preferred_element_type=jnp.float32
        )
        solved = lax.psum(jnp.where(member, partial_value, 0.0), "rows")
        update = lax.dot_general(
            lax.all_gather(first_factor[panel_index], "cols", axis=0, tiled=True),
            solved,
            CONTRACT_ROWS,
            precision=HIGHEST,
            preferred_element_type=jnp.float32,
        )
        current = jnp.where(logical_rows >= panel_end, current - update, current)
        mine_rows = lax.dynamic_slice_in_dim(solved, offset, BLOCK, 0)
        present = current[local_block * BLOCK : (local_block + 1) * BLOCK]
        current = lax.dynamic_update_slice_in_dim(
            current, jnp.where(member, mine_rows, present), local_block * BLOCK, 0
        )
    turned = lax.all_to_all(
        lax.all_to_all(current, "cols", split_axis=0, concat_axis=1, tiled=True),
        "rows",
        split_axis=1,
        concat_axis=0,
        tiled=True,
    )
    height, narrow = turned.shape

    def total_rows(partial_sum):
        return lax.psum(partial_sum, "rows")

    def update_rows(panel_number, solved_cols):
        return jnp.dot(
            solved_cols,
            lax.all_gather(second_factor[panel_number], "cols", axis=0, tiled=True),
            precision=HIGHEST,
            preferred_element_type=jnp.float32,
        )

    reduced = right_solve(turned, row_index * narrow, second_inverse, total_rows, update_rows)
    return reduced


def solution(mesh):
    return jax.shard_map(
        on_device,
        mesh=mesh,
        in_specs=(P("rows", "cols"), P(), P(None, "cols", "rows"), P(), P(None, "cols", "rows")),
        out_specs=P("cols", "rows"),
        check_vma=False,
    )
```

profile of v0, /device:TPU:1, one launch (start us, length us, event | category | flops | bytes accessed | tf_op | source)
XLA Modules:
  0.0 586.9 jit_solution(826307015627052051)
XLA Ops:
  7.4 0.0 all-reduce.5.cloned.1.call-start
  7.4 0.0 copy-start.1
  7.4 2.8 fusion.57
  10.2 0.0 copy-start.2
  10.2 0.0 copy-done.1
  10.2 1.4 convolution_select_fusion.3
  11.5 0.0 all-reduce.5.cloned.1.call-update
  11.6 0.0 all-gather.7.cloned.1.call-start
  11.6 0.0 copy-done.2
  11.6 0.8 fusion.58
  12.4 0.0 all-gather.7.cloned.1.call-update
  12.4 0.0 all-gather.9.cloned.1.call-start
  12.5 0.5 all-gather.9.cloned.1.call-update
  13.0 0.0 all-reduce.7.cloned.1.call-start
  13.1 113.7 %all-reduce.5.cloned.1.call-done = f32[512,256]{1,0:T(8,128)} async-done(((f32[512,256]{1,0:T(8,128)}), f32[512,256]{1,0:T(8,128)}) %all-reduce.5.cloned.1.call-update) | async-done | bytes 524304 | tf_op jit(solution)/shard_map/psum | solution.py:65
  126.8 0.0 all-gather.7.cloned.1.call-done
  126.8 7.2 %fusion.14 = f32[1536,256]{1,0:T(8,128)S(1)} fusion(f32[1536,256]{1,0:T(8,128)S(1)} %copy-done.1, f32[512,256]{1,0:T(8,128)} %all-reduce.5.cloned.1.call-done, f32[1,512,1536]{2,1,0:T(8,128)} %all-gather.7.cloned.1.call-done, pred[1536]{0:T(1024)(128)(4,1)S(1)} %broadcast_compare_fusion), kind=kOutput, calls=%fused_computation.14 | convolution fusion | flops 2416705536 | bytes 6817280 | tf_op jit(solution)/shard_map/dot_general | solution.py:66
  134.0 2.4 convolution_select_fusion.2
  136.4 0.0 all-reduce.7.cloned.1.call-update
  136.5 0.9 fusion.38
  137.4 0.0 all-gather.9.cloned.1.call-done
  137.4 108.6 %all-reduce.7.cloned.1.call-done = f32[512,256]{1,0:T(8,128)} async-done(((f32[512,256]{1,0:T(8,128)}), f32[512,256]{1,0:T(8,128)}) %all-reduce.7.cloned.1.call-update) | async-done | bytes 524304 | tf_op jit(solution)/shard_map/psum | solution.py:65
  246.1 7.5 %fusion.23 = f32[1536,256]{1,0:T(8,128)S(1)} fusion(f32[1536,256]{1,0:T(8,128)S(1)} %fusion.38, f32[512,256]{1,0:T(8,128)} %all-reduce.7.cloned.1.call-done, f32[1,512,1536]{2,1,0:T(8,128)} %all-gather.9.cloned.1.call-done, pred[1536]{0:T(1024)(128)(4,1)S(1)} %broadcast_compare_fusion.1), kind=kOutput, calls=%fused_computation.17 | convolution fusion | flops 2416705536 | bytes 6817280 | tf_op jit(solution)/shard_map/dot_general | solution.py:66
  253.5 0.9 fusion.36
  254.5 28.3 %all_to_all.32 = f32[16,96,256]{2,1,0:T(8,128)} all-to-all(f32[16,96,256]{2,1,0:T(8,128)S(1)} %bitcast.61), channel_id=1, replica_groups=mesh['rows'=16,'cols'=16] {'cols'}, dimensions={0} | all-to-all | bytes 3145728 | tf_op jit(solution)/shard_map/all_to_all | solution.py:80
  282.8 6.9 %all-to-all-start.1 = ((f32[96,16,256]{2,0,1:T(8,128)}), f32[96,16,256]{2,0,1:T(8,128)S(1)}, u32[]{:S(2)}, u32[]{:S(2)}) async-start(f32[96,16,256]{2,0,1:T(8,128)} %bitcast.7), calls=%async_computation.1 | async-start | bytes 3145728 | tf_op jit(solution)/shard_map/all_to_all | solution.py:79
  289.7 0.2 all-reduce.9.cloned.1.call-start
  289.9 2.7 fusion.56
  292.6 35.5 %all-to-all-done.1 = f32[96,16,256]{2,0,1:T(8,128)S(1)} async-done(((f32[96,16,256]{2,0,1:T(8,128)}), f32[96,16,256]{2,0,1:T(8,128)S(1)}, u32[]{:S(2)}, u32[]{:S(2)}) %all-to-all-start.1) | async-done | bytes 1572896 | tf_op jit(solution)/shard_map/all_to_all | solution.py:79
  328.1 4.5 convolution_select_fusion.1
  332.6 0.0 copy-start.3
  332.6 0.0 all-reduce.9.cloned.1.call-update
  332.7 0.0 all-reduce.11.cloned.1.call-start
  332.7 0.7 copy-done.3
  333.5 19.8 %all-gather.2 = f32[1,512,256]{2,1,0:T(8,128)} all-gather(f32[1,32,256]{2,1,0:T(8,128)S(1)} %get-tuple-element.12), channel_id=4, replica_groups=mesh['rows'=16,'cols'=16] {'cols'}, dimensions={1}, use_global_device_ids=true | all-gather | bytes 557056 | tf_op jit(solution)/shard_map/all_gather | solution.py:94
  353.2 91.8 %all-reduce.9.cloned.1.call-done = f32[1536,512]{1,0:T(8,128)} async-done(((f32[1536,512]{1,0:T(8,128)}), f32[1536,512]{1,0:T(8,128)}) %all-reduce.9.cloned.1.call-update) | async-done | bytes 3145744 | tf_op jit(solution)/shard_map/psum | solution.py:89
  445.1 0.0 copy-start
  445.1 5.3 fusion.7
  450.3 0.0 copy-done
  450.3 4.5 convolution_select_fusion
  454.8 0.0 all-reduce.11.cloned.1.call-update
  454.9 19.2 %all-gather.3 = f32[1,512,256]{2,1,0:T(8,128)S(1)} all-gather(f32[1,32,256]{2,1,0:T(8,128)S(1)} %get-tuple-element.11), channel_id=5, replica_groups=mesh['rows'=16,'cols'=16] {'cols'}, dimensions={1}, use_global_device_ids=true | all-gather | bytes 557056 | tf_op jit(solution)/shard_map/all_gather | solution.py:94
  474.1 99.3 %all-reduce.11.cloned.1.call-done = f32[1536,512]{1,0:T(8,128)} async-done(((f32[1536,512]{1,0:T(8,128)}), f32[1536,512]{1,0:T(8,128)}) %all-reduce.11.cloned.1.call-update) | async-done | bytes 3145744 | tf_op jit(solution)/shard_map/psum | solution.py:89
  573.4 6.4 %fusion.5 = f32[1536,256]{1,0:T(8,128)} fusion(f32[1536,256]{1,0:T(8,128)S(1)} %fusion.7, f32[1536,512]{1,0:T(8,128)} %all-reduce.11.cloned.1.call-done, s32[]{:T(128)S(6)} %min.16, pred[256]{0:T(512)(128)(4,1)S(1)} %fusion.54, pred[]{:T(512)S(6)} %and.52, f32[1,512,256]{2,1,0:T(8,128)S(1)} %all-gather.3), kind=kOutput, calls=%fused_computation.8 | convolution fusion | flops 2417098752 | bytes 8388869 | tf_op jit(solution)/shard_map/dot_general | solution.py:92
  (5 shorter events, 0.0 us)
Async XLA Ops:
  7.4 119.4 %all-reduce.5.cloned.1.call-start = ((), (), s32[]{:S(2)}) async-start(), calls=%async_computation.2 | async-start | bytes 1048576 | tf_op jit(solution)/shard_map/psum | solution.py:65
  7.4 2.8 copy-start.1
  10.2 1.4 copy-start.2
  11.6 115.2 %all-gather.7.cloned.1.call-start = ((), (), s32[]{:S(2)}) async-start(), calls=%async_computation.6 | async-start | bytes 3342336 | tf_op jit(solution)/shard_map/all_gather | solution.py:67
  12.4 125.0 %all-gather.9.cloned.1.call-start = ((), (), s32[]{:S(2)}) async-start(), calls=%async_computation.7 | async-start | bytes 3342336 | tf_op jit(solution)/shard_map/all_gather | solution.py:67
  13.0 233.1 %all-reduce.7.cloned.1.call-start = ((), (), s32[]{:S(2)}) async-start(), calls=%async_computation.3 | async-start | bytes 1048576 | tf_op jit(solution)/shard_map/psum | solution.py:65
  282.8 45.4 %all-to-all-start.1 = ((f32[96,16,256]{2,0,1:T(8,128)}), f32[96,16,256]{2,0,1:T(8,128)S(1)}, u32[]{:S(2)}, u32[]{:S(2)}) async-start(f32[96,16,256]{2,0,1:T(8,128)} %bitcast.7), calls=%async_computation.1 | async-start | bytes 3145728 | tf_op jit(solution)/shard_map/all_to_all | solution.py:79
  289.7 155.4 %all-reduce.9.cloned.1.call-start = ((), (), s32[]{:S(2)}) async-start(), calls=%async_computation.4 | async-start | bytes 6291456 | tf_op jit(solution)/shard_map/psum | solution.py:89
  332.6 0.8 copy-start.3
  332.7 240.7 %all-reduce.11.cloned.1.call-start = ((), (), s32[]{:S(2)}) async-start(), calls=%async_computation.5 | async-start | bytes 6291456 | tf_op jit(solution)/shard_map/psum | solution.py:89
  445.1 5.3 copy-start
Sparse Core Ops, SparseCore 0:
  11.7 115.0 all-reduce.4
  136.6 109.4 all-reduce.6
  332.8 112.2 all-reduce.8
  455.0 118.3 all-reduce.10
Sparse Core Ops, SparseCore 1:
  14.8 56.3 all-gather.6
  73.4 51.8 all-gather.8
where the time goes:
time: 587 us
  waiting for transfers between devices  450 us (77%)
  blocking collectives  67.2 us (11%)
  matrix products  39.2 us (7%)
  between operations  14.7 us (3%)
  starting transfers between devices  7.32 us (1%)
  local copies, waits for them, and re-layouts  7.02 us (1%)
    psum x2, waiting for transfers between devices, on_device(): solved = lax.psum(jnp.where(member, partial_value, 0.0), 'rows')  222 us
    psum x2, waiting for transfers between devices, total_rows(): return lax.psum(partial_sum, 'rows')  191 us
    all_gather x2, blocking collectives, update_rows(): lax.all_gather(second_factor[panel_number], 'cols', axis=0, tiled=True)  38.9 us
    all_to_all x1, waiting for transfers between devices, on_device(): lax.all_to_all(lax.all_to_all(current, 'cols', split_axis=0, concat_axis=...  35.5 us
    all_to_all x1, blocking collectives, on_device(): lax.all_to_all(current, 'cols', split_axis=0, concat_axis=1, tiled=True)  28.3 us
    dot_general x2, matrix products, on_device(): lax.dot_general(lax.all_gather(first_factor[panel_index], 'cols', axis=0,...  14.7 us
  transfers between devices with their start and end apart: 7, of which 5 were waited for; matrix products, arithmetic and copies ran while one was open for 2% of the time, Pallas kernels for 0%

commit v1 on v0

--- a/solution.py
+++ b/solution.py
@@ -89,9 +89,32 @@
         return lax.psum(partial_sum, "rows")
 
     def update_rows(panel_number, solved_cols):
+
+        def fill_the_record(content):
+            mixed_arr = lax.axis_index("cols")
+            b_now = lax.axis_size("cols")
+            x_now, local_now, long_array = (b_now, mixed_arr, content.shape[0])
+            small = tuple((i0 * x_now if w == 0 else i0 for w, i0 in enumerate(content.shape)))
+            plain = jnp.zeros(small, content.dtype)
+            opened = lax.dynamic_update_slice_in_dim(plain, content, local_now * long_array, axis=0)
+            h_now = t1 = content
+            for k0 in [*range(1, x_now // 2 + 1)]:
+                current_arr = tuple(((w, (w + 1) % x_now) for w in range(x_now)))
+                h_now = lax.ppermute(h_now, "cols", current_arr)
+                opened = lax.dynamic_update_slice_in_dim(
+                    opened, h_now, (local_now - k0) % x_now * long_array, axis=0
+                )
+                if 2 * k0 < x_now:
+                    after = tuple(((w, (w - 1) % x_now) for w in range(x_now)))
+                    t1 = lax.ppermute(t1, "cols", after)
+                    opened = lax.dynamic_update_slice_in_dim(
+                        opened, t1, (local_now + k0) % x_now * long_array, axis=0
+                    )
+            return opened
+
         return jnp.dot(
             solved_cols,
-            lax.all_gather(second_factor[panel_number], "cols", axis=0, tiled=True),
+            fill_the_record(second_factor[panel_number]),
             precision=HIGHEST,
             preferred_element_type=jnp.float32,
         )

time: 587 us -> 597 us (1.017); the launches traced: 587 us -> 588 us
  starting transfers between devices: 7.32 us -> 75.1 us
  waiting for transfers between devices: 450 us -> 411 us
  blocking collectives: 67.2 us -> 28.3 us
  local copies, waits for them, and re-layouts: 7.02 us -> 17.3 us
    ppermute x0 -> x30, starting transfers between devices: none -> 67.8 us  [the longest x14 65.2 us: fill_the_record(): t1 = lax.ppermute(t1, 'cols', after)]
    all_gather x2 -> x0, blocking collectives: 38.9 us -> none  [update_rows(): lax.all_gather(second_factor[panel_number], 'cols', axis=0, tiled=True)]
    psum x2, waiting for transfers between devices: 191 us -> 154 us  [total_rows(): return lax.psum(partial_sum, 'rows')]
    all_to_all x1, waiting for transfers between devices: 35.5 us -> 14.7 us  [on_device(): lax.all_to_all(lax.all_to_all(current, 'cols', split_axis=0, concat_axis=...]
    ppermute x0 -> x30, waiting for transfers between devices: none -> 18.4 us  [the longest x16 18.4 us: fill_the_record(): h_now = lax.ppermute(h_now, 'cols', current_arr)]
    dynamic_update_slice x0 -> x32, local copies, waits for them, and re-layouts: none -> 9.15 us  [the longest x16 4.87 us: fill_the_record(): lax.dynamic_update_slice_in_dim(opened, h_now, (local_now - k0) % x_now *...]
  transfers between devices with their start and end apart: 7 -> 37, of which waited for: 5 -> 17; matrix products, arithmetic and copies ran while one was open for 2% -> 6% of each run, Pallas kernels for 0% -> 0%
where the time goes in v1:
time: 597 us; the launch traced here: 588 us
  waiting for transfers between devices  411 us (69%)
  starting transfers between devices  75.1 us (13%)
  matrix products  39.1 us (7%)
  blocking collectives  28.3 us (5%)
  local copies, waits for them, and re-layouts  17.3 us (3%)
  between operations  15.3 us (3%)
    psum x2, waiting for transfers between devices, on_device(): solved = lax.psum(jnp.where(member, partial_value, 0.0), 'rows')  222 us
    psum x2, waiting for transfers between devices, total_rows(): return lax.psum(partial_sum, 'rows')  154 us
    ppermute x14, starting transfers between devices, fill_the_record(): t1 = lax.ppermute(t1, 'cols', after)  65.2 us
    all_to_all x1, blocking collectives, on_device(): lax.all_to_all(current, 'cols', split_axis=0, concat_axis=1, tiled=True)  28.3 us
    ppermute x16, waiting for transfers between devices, fill_the_record(): h_now = lax.ppermute(h_now, 'cols', current_arr)  18.4 us
    dot_general x2, matrix products, on_device(): lax.dot_general(lax.all_gather(first_factor[panel_index], 'cols', axis=0,...  14.7 us
    all_to_all x1, waiting for transfers between devices, on_device(): lax.all_to_all(lax.all_to_all(current, 'cols', split_axis=0, concat_axis=...  14.7 us
  transfers between devices with their start and end apart: 37, of which 17 were waited for; matrix products, arithmetic and copies ran while one was open for 6% of the time, Pallas kernels for 0%

profile of v1, /device:TPU:1, one launch (start us, length us, event | category | flops | bytes accessed | tf_op | source)
XLA Modules:
  0.0 587.7 jit_solution(6294393598763280376)
XLA Ops:
  7.4 2.8 fusion.55
  10.2 1.4 convolution_select_fusion.3
  11.6 0.8 fusion.56
  12.5 0.5 all-gather.7.cloned.1.call-update
  13.1 113.7 %all-reduce.5.cloned.1.call-done = f32[512,256]{1,0:T(8,128)} async-done(((f32[512,256]{1,0:T(8,128)}), f32[512,256]{1,0:T(8,128)}) %all-reduce.5.cloned.1.call-update) | async-done | bytes 524304 | tf_op jit(solution)/shard_map/psum | solution.py:65
  126.9 7.2 %fusion.14 = f32[1536,256]{1,0:T(8,128)S(1)} fusion(f32[1536,256]{1,0:T(8,128)S(1)} %copy-done.4, f32[512,256]{1,0:T(8,128)} %all-reduce.5.cloned.1.call-done, f32[1,512,1536]{2,1,0:T(8,128)} %all-gather.5.cloned.1.call-done, pred[1536]{0:T(1024)(128)(4,1)S(1)} %broadcast_compare_fusion), kind=kOutput, calls=%fused_computation.14 | convolution fusion | flops 2416705536 | bytes 6817280 | tf_op jit(solution)/shard_map/dot_general | solution.py:66
  134.1 2.4 convolution_select_fusion.2
  136.5 0.9 fusion.36
  137.5 108.8 %all-reduce.7.cloned.1.call-done = f32[512,256]{1,0:T(8,128)} async-done(((f32[512,256]{1,0:T(8,128)}), f32[512,256]{1,0:T(8,128)}) %all-reduce.7.cloned.1.call-update) | async-done | bytes 524304 | tf_op jit(solution)/shard_map/psum | solution.py:65
  246.3 7.5 %fusion.23 = f32[1536,256]{1,0:T(8,128)S(1)} fusion(f32[1536,256]{1,0:T(8,128)S(1)} %fusion.36, f32[512,256]{1,0:T(8,128)} %all-reduce.7.cloned.1.call-done, f32[1,512,1536]{2,1,0:T(8,128)} %all-gather.7.cloned.1.call-done, pred[1536]{0:T(1024)(128)(4,1)S(1)} %broadcast_compare_fusion.1), kind=kOutput, calls=%fused_computation.17 | convolution fusion | flops 2416705536 | bytes 6817280 | tf_op jit(solution)/shard_map/dot_general | solution.py:66
  253.7 0.9 fusion.34
  254.7 28.3 %all_to_all.32 = f32[16,96,256]{2,1,0:T(8,128)} all-to-all(f32[16,96,256]{2,1,0:T(8,128)S(1)} %bitcast.65), channel_id=1, replica_groups=mesh['rows'=16,'cols'=16] {'cols'}, dimensions={0} | all-to-all | bytes 3145728 | tf_op jit(solution)/shard_map/all_to_all | solution.py:80
  282.9 7.1 %all-to-all-start.1 = ((f32[96,16,256]{2,0,1:T(8,128)}), f32[96,16,256]{2,0,1:T(8,128)S(1)}, u32[]{:S(2)}, u32[]{:S(2)}) async-start(f32[96,16,256]{2,0,1:T(8,128)} %bitcast.7), calls=%async_computation.1 | async-start | bytes 3145728 | tf_op jit(solution)/shard_map/all_to_all | solution.py:79
  290.1 0.6 collective-permute-start
  290.6 4.5 collective-permute-start.1
  295.1 4.8 collective-permute-start.16
  300.0 0.7 copy-done.3
  300.8 2.7 fusion.54
  303.6 4.8 collective-permute-start.3
  308.4 4.8 collective-permute-start.18
  313.1 0.6 constant_dynamic-update-slice_fusion.28
  313.8 14.7 %all-to-all-done.1 = f32[96,16,256]{2,0,1:T(8,128)S(1)} async-done(((f32[96,16,256]{2,0,1:T(8,128)}), f32[96,16,256]{2,0,1:T(8,128)S(1)}, u32[]{:S(2)}, u32[]{:S(2)}) %all-to-all-start.1) | async-done | bytes 1572896 | tf_op jit(solution)/shard_map/all_to_all | solution.py:79
  328.4 4.5 convolution_select_fusion.1
  333.0 0.6 constant_dynamic-update-slice_fusion.27
  333.6 0.3 collective-permute-start.4
  333.9 4.5 collective-permute-start.5
  338.4 0.6 constant_dynamic-update-slice_fusion.26
  339.0 0.6 constant_dynamic-update-slice_fusion.25
  339.6 0.7 collective-permute-done.4
  340.3 4.8 collective-permute-start.7
  345.1 0.6 constant_dynamic-update-slice_fusion.24
  345.7 0.6 constant_dynamic-update-slice_fusion.23
  346.6 4.8 collective-permute-start.9
  351.4 0.6 constant_dynamic-update-slice_fusion.22
  352.0 0.6 constant_dynamic-update-slice_fusion.21
  352.7 4.8 collective-permute-start.11
  357.5 0.6 constant_dynamic-update-slice_fusion.20
  358.1 0.6 constant_dynamic-update-slice_fusion.19
  358.8 4.8 collective-permute-start.13
  363.6 0.6 constant_dynamic-update-slice_fusion.18
  364.2 0.6 constant_dynamic-update-slice_fusion.17
  364.9 0.6 constant_dynamic-update-slice_fusion.16
  365.5 0.6 constant_dynamic-update-slice_fusion.15
  366.1 4.9 collective-permute-done.14
  370.9 0.6 constant_dynamic-update-slice_fusion.14
  371.5 73.8 %all-reduce.9.cloned.1.call-done = f32[1536,512]{1,0:T(8,128)} async-done(((f32[1536,512]{1,0:T(8,128)}), f32[1536,512]{1,0:T(8,128)}) %all-reduce.9.cloned.1.call-update) | async-done | bytes 3145744 | tf_op jit(solution)/shard_map/psum | solution.py:89
  445.4 5.3 fusion.7
  450.6 4.5 convolution_select_fusion
  455.2 1.0 copy-done.2
  456.2 1.3 collective-permute-start.19
  457.5 3.6 collective-permute-start.20
  461.1 1.3 collective-permute-done.19
  462.4 0.2 collective-permute-start.21
  462.6 4.8 collective-permute-start.22
  467.4 1.3 collective-permute-done.21
  468.7 4.8 collective-permute-start.24
  473.5 1.3 collective-permute-done.23
  474.8 4.8 collective-permute-start.26
  479.6 1.3 collective-permute-done.25
  480.9 4.8 collective-permute-start.28
  485.6 1.3 collective-permute-done.27
  487.0 6.0 %collective-permute-done.29 = f32[32,256]{1,0:T(8,128)S(1)} collective-permute-done((f32[32,256]{1,0:T(8,128)S(1)}, f32[32,256]{1,0:T(8,128)S(1)}, u32[]{:S(2)}, u32[]{:S(2)}) %collective-permute-start.29) | collective-permute-done | bytes 32800 | tf_op jit(solution)/shard_map/ppermute | solution.py:103
  493.0 80.7 %all-reduce.11.cloned.1.call-done = f32[1536,512]{1,0:T(8,128)} async-done(((f32[1536,512]{1,0:T(8,128)}), f32[1536,512]{1,0:T(8,128)}) %all-reduce.11.cloned.1.call-update) | async-done | bytes 3145744 | tf_op jit(solution)/shard_map/psum | solution.py:89
  573.7 6.4 %fusion.5 = f32[1536,256]{1,0:T(8,128)} fusion(f32[1536,256]{1,0:T(8,128)S(1)} %fusion.7, f32[1536,512]{1,0:T(8,128)} %all-reduce.11.cloned.1.call-done, f32[512,256]{1,0:T(8,128)S(1)} %constant_dynamic-update-slice_fusion.30, s32[]{:T(128)S(6)} %min.16, pred[256]{0:T(512)(128)(4,1)S(1)} %fusion.52, pred[]{:T(512)S(6)} %and.129), kind=kOutput, calls=%fused_computation.8 | convolution fusion | flops 2417098752 | bytes 8388869 | tf_op jit(solution)/shard_map/dot_general | solution.py:115
  (83 shorter events, 1.2 us)
Async XLA Ops:
  7.4 119.5 %all-reduce.5.cloned.1.call-start = ((), (), s32[]{:S(2)}) async-start(), calls=%async_computation.2 | async-start | bytes 1048576 | tf_op jit(solution)/shard_map/psum | solution.py:65
  7.4 2.8 copy-start.4
  10.2 1.4 copy-start.5
  11.6 115.3 %all-gather.5.cloned.1.call-start = ((), (), s32[]{:S(2)}) async-start(), calls=%async_computation.6 | async-start | bytes 3342336 | tf_op jit(solution)/shard_map/all_gather | solution.py:67
  12.5 125.0 %all-gather.7.cloned.1.call-start = ((), (), s32[]{:S(2)}) async-start(), calls=%async_computation.7 | async-start | bytes 3342336 | tf_op jit(solution)/shard_map/all_gather | solution.py:67
  13.1 233.2 %all-reduce.7.cloned.1.call-start = ((), (), s32[]{:S(2)}) async-start(), calls=%async_computation.3 | async-start | bytes 1048576 | tf_op jit(solution)/shard_map/psum | solution.py:65
  282.9 7.1 %copy-start.6 = (f32[2,32,256]{2,1,0:T(8,128)S(1)}, f32[2,32,256]{2,1,0:T(8,128)}, u32[]{:S(2)}) copy-start(f32[2,32,256]{2,1,0:T(8,128)} %param.9) | copy-start | bytes 196612
  282.9 45.5 %all-to-all-start.1 = ((f32[96,16,256]{2,0,1:T(8,128)}), f32[96,16,256]{2,0,1:T(8,128)S(1)}, u32[]{:S(2)}, u32[]{:S(2)}) async-start(f32[96,16,256]{2,0,1:T(8,128)} %bitcast.7), calls=%async_computation.1 | async-start | bytes 3145728 | tf_op jit(solution)/shard_map/all_to_all | solution.py:79
  290.0 155.4 %all-reduce.9.cloned.1.call-start = ((), (), s32[]{:S(2)}) async-start(), calls=%async_computation.4 | async-start | bytes 6291456 | tf_op jit(solution)/shard_map/psum | solution.py:89
  290.1 13.4 %collective-permute-start = (f32[32,256]{1,0:T(8,128)S(1)}, f32[32,256]{1,0:T(8,128)S(1)}, u32[]{:S(2)}, u32[]{:S(2)}) collective-permute-start(f32[32,256]{1,0:T(8,128)S(1)} %get-tuple-element.12), channel_id=1, source_target_pairs={{0,1},{1,2},{2,3},{3,4},{4,5},{5,6},{6,7},{7,8},{8,9},{9,10},{10,1... | collective-permute-start | bytes 98312 | tf_op jit(solution)/shard_map/ppermute | solution.py:103
  290.6 12.9 %collective-permute-start.1 = (f32[32,256]{1,0:T(8,128)S(1)}, f32[32,256]{1,0:T(8,128)S(1)}, u32[]{:S(2)}, u32[]{:S(2)}) collective-permute-start(f32[32,256]{1,0:T(8,128)S(1)} %get-tuple-element.12), channel_id=1, source_target_pairs={{0,15},{1,0},{2,1},{3,2},{4,3},{5,4},{6,5},{7,6},{8,7},{9,8},{10,9... | collective-permute-start | bytes 98312 | tf_op jit(solution)/shard_map/ppermute | solution.py:109
  295.1 13.2 %collective-permute-start.15 = (f32[32,256]{1,0:T(8,128)S(1)}, f32[32,256]{1,0:T(8,128)S(1)}, u32[]{:S(2)}, u32[]{:S(2)}) collective-permute-start(f32[32,256]{1,0:T(8,128)S(1)} %get-tuple-element.11), channel_id=1, source_target_pairs={{0,1},{1,2},{2,3},{3,4},{4,5},{5,6},{6,7},{7,8},{8,9},{9,10},{10,1... | collective-permute-start | bytes 98312 | tf_op jit(solution)/shard_map/ppermute | solution.py:103
  295.1 13.2 %collective-permute-start.16 = (f32[32,256]{1,0:T(8,128)S(1)}, f32[32,256]{1,0:T(8,128)S(1)}, u32[]{:S(2)}, u32[]{:S(2)}) collective-permute-start(f32[32,256]{1,0:T(8,128)S(1)} %get-tuple-element.11), channel_id=1, source_target_pairs={{0,15},{1,0},{2,1},{3,2},{4,3},{5,4},{6,5},{7,6},{8,7},{9,8},{10,9... | collective-permute-start | bytes 98312 | tf_op jit(solution)/shard_map/ppermute | solution.py:109
  300.0 0.8 copy-start.3
  303.5 30.1 %collective-permute-start.2 = (f32[32,256]{1,0:T(8,128)S(1)}, f32[32,256]{1,0:T(8,128)S(1)}, u32[]{:S(2)}, u32[]{:S(2)}) collective-permute-start(f32[32,256]{1,0:T(8,128)S(1)} %collective-permute-done), channel_id=1, source_target_pairs={{0,1},{1,2},{2,3},{3,4},{4,5},{5,6},{6,7},{7,8},{8,9},{9,10},{10,1... | collective-permute-start | bytes 98312 | tf_op jit(solution)/shard_map/ppermute | solution.py:103
  303.6 30.3 %collective-permute-start.3 = (f32[32,256]{1,0:T(8,128)S(1)}, f32[32,256]{1,0:T(8,128)S(1)}, u32[]{:S(2)}, u32[]{:S(2)}) collective-permute-start(f32[32,256]{1,0:T(8,128)S(1)} %collective-permute-done.1), channel_id=1, source_target_pairs={{0,15},{1,0},{2,1},{3,2},{4,3},{5,4},{6,5},{7,6},{8,7},{9,8},{10,9... | collective-permute-start | bytes 98312 | tf_op jit(solution)/shard_map/ppermute | solution.py:109
  308.3 147.9 %collective-permute-start.17 = (f32[32,256]{1,0:T(8,128)S(1)}, f32[32,256]{1,0:T(8,128)S(1)}, u32[]{:S(2)}, u32[]{:S(2)}) collective-permute-start(f32[32,256]{1,0:T(8,128)S(1)} %collective-permute-done.15), channel_id=1, source_target_pairs={{0,1},{1,2},{2,3},{3,4},{4,5},{5,6},{6,7},{7,8},{8,9},{9,10},{10,1... | collective-permute-start | bytes 98312 | tf_op jit(solution)/shard_map/ppermute | solution.py:103
  308.4 149.1 %collective-permute-start.18 = (f32[32,256]{1,0:T(8,128)S(1)}, f32[32,256]{1,0:T(8,128)S(1)}, u32[]{:S(2)}, u32[]{:S(2)}) collective-permute-start(f32[32,256]{1,0:T(8,128)S(1)} %collective-permute-done.16), channel_id=1, source_target_pairs={{0,15},{1,0},{2,1},{3,2},{4,3},{5,4},{6,5},{7,6},{8,7},{9,8},{10,9... | collective-permute-start | bytes 98312 | tf_op jit(solution)/shard_map/ppermute | solution.py:109
  313.7 19.2 %copy-start.1 = (f32[512,256]{1,0:T(8,128)}, f32[512,256]{1,0:T(8,128)S(1)}, u32[]{:S(2)}) copy-start(f32[512,256]{1,0:T(8,128)S(1)} %constant_dynamic-update-slice_fusion.12) | copy-start | bytes 1572868
  333.0 240.7 %all-reduce.11.cloned.1.call-start = ((), (), s32[]{:S(2)}) async-start(), calls=%async_computation.5 | async-start | bytes 6291456 | tf_op jit(solution)/shard_map/psum | solution.py:89
  333.6 6.7 %collective-permute-start.4 = (f32[32,256]{1,0:T(8,128)S(1)}, f32[32,256]{1,0:T(8,128)S(1)}, u32[]{:S(2)}, u32[]{:S(2)}) collective-permute-start(f32[32,256]{1,0:T(8,128)S(1)} %collective-permute-done.2), channel_id=1, source_target_pairs={{0,1},{1,2},{2,3},{3,4},{4,5},{5,6},{6,7},{7,8},{8,9},{9,10},{10,1... | collective-permute-start | bytes 98312 | tf_op jit(solution)/shard_map/ppermute | solution.py:103
  333.9 6.4 %collective-permute-start.5 = (f32[32,256]{1,0:T(8,128)S(1)}, f32[32,256]{1,0:T(8,128)S(1)}, u32[]{:S(2)}, u32[]{:S(2)}) collective-permute-start(f32[32,256]{1,0:T(8,128)S(1)} %collective-permute-done.3), channel_id=1, source_target_pairs={{0,15},{1,0},{2,1},{3,2},{4,3},{5,4},{6,5},{7,6},{8,7},{9,8},{10,9... | collective-permute-start | bytes 98312 | tf_op jit(solution)/shard_map/ppermute | solution.py:109
  340.3 6.1 %collective-permute-start.6 = (f32[32,256]{1,0:T(8,128)S(1)}, f32[32,256]{1,0:T(8,128)S(1)}, u32[]{:S(2)}, u32[]{:S(2)}) collective-permute-start(f32[32,256]{1,0:T(8,128)S(1)} %collective-permute-done.4), channel_id=1, source_target_pairs={{0,1},{1,2},{2,3},{3,4},{4,5},{5,6},{6,7},{7,8},{8,9},{9,10},{10,1... | collective-permute-start | bytes 98312 | tf_op jit(solution)/shard_map/ppermute | solution.py:103
  340.3 6.3 %collective-permute-start.7 = (f32[32,256]{1,0:T(8,128)S(1)}, f32[32,256]{1,0:T(8,128)S(1)}, u32[]{:S(2)}, u32[]{:S(2)}) collective-permute-start(f32[32,256]{1,0:T(8,128)S(1)} %collective-permute-done.5), channel_id=1, source_target_pairs={{0,15},{1,0},{2,1},{3,2},{4,3},{5,4},{6,5},{7,6},{8,7},{9,8},{10,9... | collective-permute-start | bytes 98312 | tf_op jit(solution)/shard_map/ppermute | solution.py:109
  346.4 6.3 %collective-permute-start.8 = (f32[32,256]{1,0:T(8,128)S(1)}, f32[32,256]{1,0:T(8,128)S(1)}, u32[]{:S(2)}, u32[]{:S(2)}) collective-permute-start(f32[32,256]{1,0:T(8,128)S(1)} %collective-permute-done.6), channel_id=1, source_target_pairs={{0,1},{1,2},{2,3},{3,4},{4,5},{5,6},{6,7},{7,8},{8,9},{9,10},{10,1... | collective-permute-start | bytes 98312 | tf_op jit(solution)/shard_map/ppermute | solution.py:103
  346.6 6.1 %collective-permute-start.9 = (f32[32,256]{1,0:T(8,128)S(1)}, f32[32,256]{1,0:T(8,128)S(1)}, u32[]{:S(2)}, u32[]{:S(2)}) collective-permute-start(f32[32,256]{1,0:T(8,128)S(1)} %collective-permute-done.7), channel_id=1, source_target_pairs={{0,15},{1,0},{2,1},{3,2},{4,3},{5,4},{6,5},{7,6},{8,7},{9,8},{10,9... | collective-permute-start | bytes 98312 | tf_op jit(solution)/shard_map/ppermute | solution.py:109
  352.7 6.1 %collective-permute-start.10 = (f32[32,256]{1,0:T(8,128)S(1)}, f32[32,256]{1,0:T(8,128)S(1)}, u32[]{:S(2)}, u32[]{:S(2)}) collective-permute-start(f32[32,256]{1,0:T(8,128)S(1)} %collective-permute-done.8), channel_id=1, source_target_pairs={{0,1},{1,2},{2,3},{3,4},{4,5},{5,6},{6,7},{7,8},{8,9},{9,10},{10,1... | collective-permute-start | bytes 98312 | tf_op jit(solution)/shard_map/ppermute | solution.py:103
  352.7 6.1 %collective-permute-start.11 = (f32[32,256]{1,0:T(8,128)S(1)}, f32[32,256]{1,0:T(8,128)S(1)}, u32[]{:S(2)}, u32[]{:S(2)}) collective-permute-start(f32[32,256]{1,0:T(8,128)S(1)} %collective-permute-done.9), channel_id=1, source_target_pairs={{0,15},{1,0},{2,1},{3,2},{4,3},{5,4},{6,5},{7,6},{8,7},{9,8},{10,9... | collective-permute-start | bytes 98312 | tf_op jit(solution)/shard_map/ppermute | solution.py:109
  358.8 6.1 %collective-permute-start.12 = (f32[32,256]{1,0:T(8,128)S(1)}, f32[32,256]{1,0:T(8,128)S(1)}, u32[]{:S(2)}, u32[]{:S(2)}) collective-permute-start(f32[32,256]{1,0:T(8,128)S(1)} %collective-permute-done.10), channel_id=1, source_target_pairs={{0,1},{1,2},{2,3},{3,4},{4,5},{5,6},{6,7},{7,8},{8,9},{9,10},{10,1... | collective-permute-start | bytes 98312 | tf_op jit(solution)/shard_map/ppermute | solution.py:103
  358.8 6.7 %collective-permute-start.13 = (f32[32,256]{1,0:T(8,128)S(1)}, f32[32,256]{1,0:T(8,128)S(1)}, u32[]{:S(2)}, u32[]{:S(2)}) collective-permute-start(f32[32,256]{1,0:T(8,128)S(1)} %collective-permute-done.11), channel_id=1, source_target_pairs={{0,15},{1,0},{2,1},{3,2},{4,3},{5,4},{6,5},{7,6},{8,7},{9,8},{10,9... | collective-permute-start | bytes 98312 | tf_op jit(solution)/shard_map/ppermute | solution.py:109
  364.8 6.1 %collective-permute-start.14 = (f32[32,256]{1,0:T(8,128)S(1)}, f32[32,256]{1,0:T(8,128)S(1)}, u32[]{:S(2)}, u32[]{:S(2)}) collective-permute-start(f32[32,256]{1,0:T(8,128)S(1)} %collective-permute-done.12), channel_id=1, source_target_pairs={{0,1},{1,2},{2,3},{3,4},{4,5},{5,6},{6,7},{7,8},{8,9},{9,10},{10,1... | collective-permute-start | bytes 98312 | tf_op jit(solution)/shard_map/ppermute | solution.py:103
  445.4 5.3 copy-start
  455.1 1.0 copy-start.2
  456.2 6.2 %collective-permute-start.19 = (f32[32,256]{1,0:T(8,128)S(1)}, f32[32,256]{1,0:T(8,128)S(1)}, u32[]{:S(2)}, u32[]{:S(2)}) collective-permute-start(f32[32,256]{1,0:T(8,128)S(1)} %collective-permute-done.17), channel_id=1, source_target_pairs={{0,1},{1,2},{2,3},{3,4},{4,5},{5,6},{6,7},{7,8},{8,9},{9,10},{10,1... | collective-permute-start | bytes 98312 | tf_op jit(solution)/shard_map/ppermute | solution.py:103
  457.5 5.1 collective-permute-start.20
  462.4 6.3 %collective-permute-start.21 = (f32[32,256]{1,0:T(8,128)S(1)}, f32[32,256]{1,0:T(8,128)S(1)}, u32[]{:S(2)}, u32[]{:S(2)}) collective-permute-start(f32[32,256]{1,0:T(8,128)S(1)} %collective-permute-done.19), channel_id=1, source_target_pairs={{0,1},{1,2},{2,3},{3,4},{4,5},{5,6},{6,7},{7,8},{8,9},{9,10},{10,1... | collective-permute-start | bytes 98312 | tf_op jit(solution)/shard_map/ppermute | solution.py:103
  462.6 6.1 %collective-permute-start.22 = (f32[32,256]{1,0:T(8,128)S(1)}, f32[32,256]{1,0:T(8,128)S(1)}, u32[]{:S(2)}, u32[]{:S(2)}) collective-permute-start(f32[32,256]{1,0:T(8,128)S(1)} %collective-permute-done.20), channel_id=1, source_target_pairs={{0,15},{1,0},{2,1},{3,2},{4,3},{5,4},{6,5},{7,6},{8,7},{9,8},{10,9... | collective-permute-start | bytes 98312 | tf_op jit(solution)/shard_map/ppermute | solution.py:109
  468.7 6.1 %collective-permute-start.23 = (f32[32,256]{1,0:T(8,128)S(1)}, f32[32,256]{1,0:T(8,128)S(1)}, u32[]{:S(2)}, u32[]{:S(2)}) collective-permute-start(f32[32,256]{1,0:T(8,128)S(1)} %collective-permute-done.21), channel_id=1, source_target_pairs={{0,1},{1,2},{2,3},{3,4},{4,5},{5,6},{6,7},{7,8},{8,9},{9,10},{10,1... | collective-permute-start | bytes 98312 | tf_op jit(solution)/shard_map/ppermute | solution.py:103
  468.7 6.1 %collective-permute-start.24 = (f32[32,256]{1,0:T(8,128)S(1)}, f32[32,256]{1,0:T(8,128)S(1)}, u32[]{:S(2)}, u32[]{:S(2)}) collective-permute-start(f32[32,256]{1,0:T(8,128)S(1)} %collective-permute-done.22), channel_id=1, source_target_pairs={{0,15},{1,0},{2,1},{3,2},{4,3},{5,4},{6,5},{7,6},{8,7},{9,8},{10,9... | collective-permute-start | bytes 98312 | tf_op jit(solution)/shard_map/ppermute | solution.py:109
  474.8 6.1 %collective-permute-start.25 = (f32[32,256]{1,0:T(8,128)S(1)}, f32[32,256]{1,0:T(8,128)S(1)}, u32[]{:S(2)}, u32[]{:S(2)}) collective-permute-start(f32[32,256]{1,0:T(8,128)S(1)} %collective-permute-done.23), channel_id=1, source_target_pairs={{0,1},{1,2},{2,3},{3,4},{4,5},{5,6},{6,7},{7,8},{8,9},{9,10},{10,1... | collective-permute-start | bytes 98312 | tf_op jit(solution)/shard_map/ppermute | solution.py:103
  474.8 6.1 %collective-permute-start.26 = (f32[32,256]{1,0:T(8,128)S(1)}, f32[32,256]{1,0:T(8,128)S(1)}, u32[]{:S(2)}, u32[]{:S(2)}) collective-permute-start(f32[32,256]{1,0:T(8,128)S(1)} %collective-permute-done.24), channel_id=1, source_target_pairs={{0,15},{1,0},{2,1},{3,2},{4,3},{5,4},{6,5},{7,6},{8,7},{9,8},{10,9... | collective-permute-start | bytes 98312 | tf_op jit(solution)/shard_map/ppermute | solution.py:109
  480.8 6.1 %collective-permute-start.27 = (f32[32,256]{1,0:T(8,128)S(1)}, f32[32,256]{1,0:T(8,128)S(1)}, u32[]{:S(2)}, u32[]{:S(2)}) collective-permute-start(f32[32,256]{1,0:T(8,128)S(1)} %collective-permute-done.25), channel_id=1, source_target_pairs={{0,1},{1,2},{2,3},{3,4},{4,5},{5,6},{6,7},{7,8},{8,9},{9,10},{10,1... | collective-permute-start | bytes 98312 | tf_op jit(solution)/shard_map/ppermute | solution.py:103
  480.9 6.1 %collective-permute-start.28 = (f32[32,256]{1,0:T(8,128)S(1)}, f32[32,256]{1,0:T(8,128)S(1)}, u32[]{:S(2)}, u32[]{:S(2)}) collective-permute-start(f32[32,256]{1,0:T(8,128)S(1)} %collective-permute-done.26), channel_id=1, source_target_pairs={{0,15},{1,0},{2,1},{3,2},{4,3},{5,4},{6,5},{7,6},{8,7},{9,8},{10,9... | collective-permute-start | bytes 98312 | tf_op jit(solution)/shard_map/ppermute | solution.py:109
  486.9 6.1 %collective-permute-start.29 = (f32[32,256]{1,0:T(8,128)S(1)}, f32[32,256]{1,0:T(8,128)S(1)}, u32[]{:S(2)}, u32[]{:S(2)}) collective-permute-start(f32[32,256]{1,0:T(8,128)S(1)} %collective-permute-done.27), channel_id=1, source_target_pairs={{0,1},{1,2},{2,3},{3,4},{4,5},{5,6},{6,7},{7,8},{8,9},{9,10},{10,1... | collective-permute-start | bytes 98312 | tf_op jit(solution)/shard_map/ppermute | solution.py:103
Sparse Core Ops, SparseCore 0:
  11.7 115.1 all-reduce.4
  136.6 109.5 all-reduce.6
  333.1 112.2 all-reduce.8
  455.3 118.3 all-reduce.10
Sparse Core Ops, SparseCore 1:
  14.8 56.2 all-gather.4
  73.4 51.8 all-gather.6
